TPU v7x, 768 devices: a whole 4x8x12 slice. The times are simulated.
768 devices in a mesh: span: 12 (over z), shard: 64 (over x, y, core).
Axes of the slice: x: 4, y: 8, z: 12, core: 2. Of those that a mesh axis runs over, the one named last changes fastest.
Arguments:
- tokens: bfloat16 [196608, 1152], P(('span', 'shard')), may hold values from -6 to 6
- out_proj: bfloat16 [1152, 1152], replicated, may hold values from -0.1875 to 0.1875
- phi_mean: float32 [1152], replicated, may hold values from -6 to 6
- phi_rotate: bfloat16 [1152, 576], replicated, may hold values from -0.1875 to 0.1875
- destinations: int32 [196608, 1], P(('span', 'shard')), may hold values from 0 to 11; in each aligned block of 256 rows (0 to 255, 256 to 511, ...) at most 32 rows name the same one
- student_hidden: bfloat16 [294912, 1280], P(('span', 'shard')), may hold values from -6 to 6
- adaptor: bfloat16 [1280, 576], replicated, may hold values from -0.15625 to 0.15625
- master: float32 [1280, 576], P('shard'), may hold values from -0.15625 to 0.15625
- moment_one: float32 [1280, 576], P('shard'), may hold values from -4 to 4
- moment_two: float32 [1280, 576], P('shard'), may hold values from 0.01 to 1
Outputs:
- updated_master: float32 [1280, 576], P('shard')
- updated_first: float32 [1280, 576], P('shard')
- updated_second: float32 [1280, 576], P('shard')
Inputs may be any that keep to these rules, and one draw needn't show every extreme that they name: `destinations`: at most 32 of the 256 rows of one device name one span; some span gets exactly 32.
All inputs are finite; a program needn't handle non-finite values.
Results may differ from a plain program's by a relative error of at most 0.00064.
Values may be sent and summed in bfloat16 or wider, within the bound.
No kernel may reach another device: no remote copies, remote signals or barrier semaphores. Data moves between devices by JAX's collectives and lax.ppermute only.
A program may use at most 64 MiB of HBM per device.

v0:
```python
import jax
import jax.numpy as jnp
from jax import lax
from jax.experimental import pallas as pl
from jax.experimental.pallas import tpu as pltpu
from jax.sharding import Mesh, PartitionSpec as P

ADAM_STEP = 1000
beta_first = 0.9
beta_second = 0.999
adam_epsilon = 1e-08
decay_rate = 0.05
learn_rate = 0.001

NZ, NX, NY, NC = 12, 4, 8, 2
CAP = 32
ROWS = 256
SLOTS = NZ * CAP
H = 1280
DW = 576
WIDE = 640
OWN = 20
XB = H // NX
YB = XB // NY
PACKED = 2 * CAP + 8
XROWS = 2 * XB + XB // 4
TILE_ROWS = NZ * 8
EMPTY = 1e30
f32 = jnp.float32
bf16 = jnp.bfloat16
NT = (((1,), (1,)), ((), ()))


def call(kernel, outs, args, scratch=(), vmem=24, specs=None, flops=0, moved=0):
    return pl.pallas_call(
        kernel,
        out_shape=outs,
        in_specs=specs or [pl.BlockSpec()] * len(args),
        scratch_shapes=list(scratch),
        compiler_params=pltpu.CompilerParams(vmem_limit_bytes=vmem * 2**20),
        cost_estimate=pl.CostEstimate(flops=flops, bytes_accessed=moved, transcendentals=0),
    )(*args)


def turn(x, by):
    by = by % 128
    return pltpu.roll(x, by, axis=x.ndim - 1) if by else x


def quarters(parts):
    lane = lax.broadcasted_iota(jnp.int32, parts[0].shape, parts[0].ndim - 1)
    out = parts[3]
    for q in (2, 1, 0):
        out = jnp.where(lane < 32 * (q + 1), parts[q], out)
    return out


def place_kernel(dest_ref, out_ref):
    dest = dest_ref[...]
    spans = lax.broadcasted_iota(jnp.int32, (16, ROWS), 0)
    one_hot = jnp.where(spans == dest, 1.0, 0.0)
    earlier = (
        lax.broadcasted_iota(jnp.int32, (ROWS, ROWS), 0)
        < lax.broadcasted_iota(jnp.int32, (ROWS, ROWS), 1)
    )
    before = jnp.dot(
        one_hot.astype(bf16),
        jnp.where(earlier, 1.0, 0.0).astype(bf16),
        preferred_element_type=f32,
    )
    rank = jnp.sum(before * one_hot, axis=0, keepdims=True)
    slot = dest * CAP + rank.astype(jnp.int32)
    place = lax.broadcasted_iota(jnp.int32, (SLOTS, ROWS), 0) == slot
    out_ref[...] = jnp.where(place, 1.0, 0.0).astype(bf16)


def spread_kernel(place_ref, rows_ref, out_ref, last_ref):
    place = place_ref[...]
    live = jnp.sum(place.astype(f32), axis=1, keepdims=True) > 0.5
    main = jnp.dot(place, rows_ref[:, :512], preferred_element_type=f32)
    main = jnp.where(live, main, EMPTY).astype(bf16)
    last = jnp.dot(place, rows_ref[:, 512:], preferred_element_type=f32)
    last_ref[:, 64:] = jnp.zeros((SLOTS, 64), f32)
    last_ref[:, :64] = jnp.where(live, last, EMPTY)
    last = last_ref[...].reshape(NZ, CAP, 128)
    for c in range(NC):
        packed = quarters(
            [turn(last[:, 8 * q : 8 * q + 8, :], 32 * (q - c)) for q in range(4)]
        ).astype(bf16)
        for z in range(NZ):
            rows = slice(z * CAP, (z + 1) * CAP)
            at = 256 * c
            out_ref[NC * z + c, 0:32, :] = main[rows, at : at + 128]
            out_ref[NC * z + c, 32:64, :] = main[rows, at + 128 : at + 256]
            out_ref[NC * z + c, 64:72, :] = packed[z]


def student_kernel(core_ref, act_ref, adaptor_t_ref, pred_ref, act_t_ref):
    core = core_ref[0]
    main = adaptor_t_ref[pl.ds(pl.multiple_of(core * 256, 256), 256), :]
    last = adaptor_t_ref[pl.ds(pl.multiple_of(512 + core * 32, 32), 32), :]
    act = act_ref[...]
    pred_ref[:, :256] = lax.dot_general(act, main, NT, preferred_element_type=f32)
    pred_ref[:, 256:] = lax.dot_general(act, last, NT, preferred_element_type=f32)
    act_t_ref[...] = act.T


def error_kernel(
    core_ref,
    arrived_ref,
    own_pred,
    own_act_t,
    other_pred,
    other_act_t,
    out_ref,
    main_t,
    last_t,
    grad_last,
):
    core = core_ref[0]

    def scaled(pred, target):
        return (jnp.where(target < 0.1 * EMPTY, pred - target, 0.0) / DW).astype(bf16)

    grad = rest = None
    for source, pred, act_t in (
        (core, own_pred, own_act_t),
        (1 - core, other_pred, other_act_t),
    ):
        for z in range(NZ):
            block = arrived_ref[NC * z + source].astype(f32)
            at = z * CAP
            main_t[at : at + CAP, 0:128] = block[0:32]
            main_t[at : at + CAP, 128:256] = block[32:64]
            for q in range(4):
                last_t[at + 8 * q : at + 8 * q + 8, :] = turn(block[64:72], -32 * q)
        units = act_t[...]
        main_part = jnp.dot(units, scaled(pred[:, :256], main_t[...]), preferred_element_type=f32)
        last_part = jnp.dot(units, scaled(pred[:, 256:], last_t[:, :32]), preferred_element_type=f32)
        grad = main_part if grad is None else grad + main_part
        rest = last_part if rest is None else rest + last_part
    grad = grad.astype(bf16)
    grad_last[:, :32] = rest
    for x in range(NX):
        at = x * XB
        out_ref[x, 0:XB, :] = grad[at : at + XB, 0:128]
        out_ref[x, XB : 2 * XB, :] = grad[at : at + XB, 128:256]
        out_ref[x, 2 * XB :, :] = quarters(
            [turn(grad_last[at + 80 * q : at + 80 * q + 80, :], 32 * q) for q in range(4)]
        ).astype(bf16)


def tile_kernel(got_ref, out_ref, sum_ref, flat_ref):
    total = got_ref[0].astype(f32)
    for x in range(1, NX):
        total = total + got_ref[x].astype(f32)
    sum_ref[...] = total
    for y in range(NY):
        to, at = y * TILE_ROWS, y * YB
        flat_ref[to : to + 40, :] = sum_ref[at : at + 40, :]
        flat_ref[to + 40 : to + 80, :] = sum_ref[XB + at : XB + at + 40, :]
        rest = 2 * XB + (y % 2) * 40
        flat_ref[to + 80 : to + 90, :] = quarters(
            [
                turn(sum_ref[rest + 10 * q : rest + 10 * q + 10, :], 32 * (q - y // 2))
                for q in range(4)
            ]
        )
        flat_ref[to + 90 : to + 96, :] = jnp.zeros((6, 128), f32)
        for z in range(NZ):
            out_ref[z * NY + y] = flat_ref[to + z * 8 : to + z * 8 + 8, :].astype(out_ref.dtype)


def adam_kernel(
    core_ref, tiles_ref, master_ref, one_ref, two_ref, m_out, f_out, s_out, grad_ref, flat_ref
):
    first_core = core_ref[0] == 0
    upper, lower = [], []
    for c in range(NC):
        base = c * TILE_ROWS
        for z in range(NZ):
            flat_ref[base + z * 8 : base + z * 8 + 8, :] = tiles_ref[NC * z + c]
        for part in range(2):
            at = base + 40 * part
            to = 256 * c + 128 * part
            grad_ref[:, to : to + 128] = jnp.where(
                first_core, flat_ref[at : at + 20, :], flat_ref[at + 20 : at + 40, :]
            )
        packed = flat_ref[base + 80 : base + 90, :]
        upper.append(jnp.where(first_core, turn(packed, 32 * c), turn(packed, 32 * c - 64)))
        lower.append(jnp.where(first_core, turn(packed, 32 * c - 32), turn(packed, 32 * c - 96)))
    left = lax.broadcasted_iota(jnp.int32, (10, 128), 1) < 32
    grad_ref[0:10, 512:640] = jnp.where(left, upper[0], upper[1])
    grad_ref[10:20, 512:640] = jnp.where(left, lower[0], lower[1])
    gradient = grad_ref[:, :DW]
    master = master_ref[...]
    first_new = beta_first * one_ref[...] + (1.0 - beta_first) * gradient
    second_new = beta_second * two_ref[...] + (1.0 - beta_second) * gradient * gradient
    bias_first = 1.0 - beta_first**ADAM_STEP
    bias_second = 1.0 - beta_second**ADAM_STEP
    update_dir = (
        first_new / bias_first / (jnp.sqrt(second_new / bias_second) + adam_epsilon)
        + decay_rate * master
    )
    m_out[...] = master - learn_rate * update_dir
    f_out[...] = first_new
    s_out[...] = second_new


def exchange(x, axis):
    return lax.all_to_all(x, axis, split_axis=0, concat_axis=0, tiled=True)


def body(
    tokens,
    out_proj,
    phi_mean,
    phi_rotate,
    destinations,
    student_hidden,
    adaptor,
    master,
    moment_one,
    moment_two,
):
    shape = jax.ShapeDtypeStruct
    whole, scalar = pl.BlockSpec(), pl.BlockSpec(memory_space=pltpu.SMEM)
    core = lax.axis_index("c").astype(jnp.int32).reshape(1)
    place = call(place_kernel, shape((SLOTS, ROWS), bf16), (destinations.reshape(1, ROWS),))
    place, tokens = lax.optimization_barrier((place, tokens))
    projected = (jnp.dot(tokens, out_proj, preferred_element_type=f32) - phi_mean).astype(bf16)
    target = jnp.dot(projected, phi_rotate, preferred_element_type=f32).astype(bf16)
    outgoing = call(
        spread_kernel,
        shape((NZ * NC, PACKED, 128), bf16),
        (place, target),
        scratch=(pltpu.VMEM((SLOTS, 128), f32),),
        flops=2 * SLOTS * ROWS * WIDE,
        moved=2 * WIDE * (SLOTS + ROWS),
    )
    arrived = exchange(outgoing, ("z", "c"))
    activated = jax.nn.gelu(student_hidden.astype(f32), approximate=False).astype(bf16)
    other = lax.ppermute(activated, "c", [(0, 1), (1, 0)])

    def student(act):
        return call(
            student_kernel,
            (shape((SLOTS, 288), f32), shape((H, SLOTS), bf16)),
            (core, act, adaptor.T),
            specs=[scalar, whole, whole],
            vmem=60,
            flops=2 * SLOTS * H * 288,
            moved=4 * SLOTS * H + 2 * H * DW + 4 * SLOTS * 384,
        )

    partial = call(
        error_kernel,
        shape((NX, XROWS, 128), bf16),
        (core, arrived, *student(activated), *student(other)),
        specs=[scalar] + [whole] * 5,
        vmem=60,
        scratch=(
            pltpu.VMEM((SLOTS, 256), f32),
            pltpu.VMEM((SLOTS, 128), f32),
            pltpu.VMEM((H, 128), f32),
        ),
        flops=4 * SLOTS * H * 384,
        moved=4 * SLOTS * H + 8 * SLOTS * 384,
    )
    by_x = exchange(partial, "x")
    tiles = call(
        tile_kernel,
        shape((NZ * NY, 8, 128), bf16),
        (by_x,),
        scratch=(pltpu.VMEM((XROWS, 128), f32), pltpu.VMEM((NY * TILE_ROWS, 128), f32)),
        moved=4 * XROWS * 128 * 4,
    )
    by_yz = exchange(tiles, ("z", "y"))
    part = by_yz.astype(f32).sum(axis=0)
    gathered = exchange(jnp.broadcast_to(part, (NZ * NC, 8, 128)), ("z", "c"))
    out = shape((OWN, DW), f32)
    return call(
        adam_kernel,
        (out, out, out),
        (core, gathered, master, moment_one, moment_two),
        specs=[scalar, whole, whole, whole, whole],
        scratch=(pltpu.VMEM((OWN, WIDE), f32), pltpu.VMEM((NC * TILE_ROWS, 128), f32)),
        moved=4 * OWN * DW * 7,
    )


def solution(mesh):
    grid = Mesh(mesh.devices.reshape(NZ, NX, NY, NC), ("z", "x", "y", "c"))
    rows = P(("z", "x", "y", "c"), None)
    state = P(("x", "y", "c"), None)
    in_specs = (rows, P(), P(), P(), rows, rows, P(), state, state, state)
    return jax.shard_map(
        body, mesh=grid, in_specs=in_specs, out_specs=(state, state, state), check_vma=False
    )
```

profile of v0, /device:TPU:1, one launch (start us, length us, event | category | flops | bytes accessed | tf_op | source)
XLA Modules:
  0.0 109.5 jit_solution(3074382921969265044)
XLA Ops:
  0.6 0.0 copy-start
  0.6 0.0 copy-start.4
  0.7 0.8 copy-done.4
  1.5 0.2 shard_map.121.place_ref
  1.7 0.7 copy-done
  2.4 3.0 %convolution_convert_fusion = bf16[256,576]{0,1:T(8,128)(2,1)S(1)} fusion(bf16[1152,576]{0,1:T(8,128)(2,1)} %param.13, bf16[256,1152]{1,0:T(8,128)(2,1)} %param.10, bf16[1152,1152]{1,0:T(8,128)(2,1)S(1)} %copy-done, f32[1152]{0:T(1024)} %param.12), kind=kOutput, calls=%fused_computation.36 | convolution fusion | flops 1019953152 | bytes 4870656 | tf_op jit(solution)/shard_map/dot_general | solution.py:232
  5.4 0.2 copy.14.rows_ref
  5.6 1.2 %shard_map.122 = bf16[24,72,128]{2,1,0:T(8,128)(2,1)} custom-call(bf16[384,256]{1,0:T(8,128)(2,1)S(1)} %shard_map.121.place_ref, bf16[256,576]{1,0:T(8,128)(2,1)S(1)} %copy.14.rows_ref), custom_call_target="tpu_custom_call" | custom-call | flops 125829120 | bytes 819200 | tf_op jit(solution)/shard_map/pallas_call | solution.py:35
  6.8 16.7 %all-to-all-start = ((bf16[24,72,128]{2,1,0:T(8,128)(2,1)}), bf16[24,72,128]{2,1,0:T(8,128)(2,1)S(1)}, u32[]{:S(2)}, u32[]{:S(2)}) async-start(bf16[24,72,128]{2,1,0:T(8,128)(2,1)} %shard_map.122), calls=%async_computation | async-start | bytes 884736 | tf_op jit(solution)/shard_map/all_to_all | solution.py:211
  23.5 6.0 %fusion.2.act_ref = bf16[384,1280]{1,0:T(8,128)(2,1)} fusion(bf16[384,1280]{1,0:T(8,128)(2,1)} %param.15), kind=kLoop, calls=%fused_computation.6 | loop fusion | flops 32440320 | bytes 1966080 | tf_op jit(solution)/shard_map/convert_element_type | solution.py:242
  29.5 2.1 %collective-permute-start = (bf16[384,1280]{1,0:T(8,128)(2,1)}, bf16[384,1280]{1,0:T(8,128)(2,1)}, u32[]{:S(2)}, u32[]{:S(2)}) collective-permute-start(bf16[384,1280]{1,0:T(8,128)(2,1)} %fusion.2.act_ref), channel_id=1, source_target_pairs={{0,1},{1,0},{2,3},{3,2},{4,5},{5,4},{6,7},{7,6},{8,9},{9,8},{10,11... | collective-permute-start | bytes 2949128 | tf_op jit(solution)/shard_map/ppermute | solution.py:243
  31.6 3.5 %shard_map.123 = (f32[384,288]{1,0:T(8,128)}, bf16[1280,384]{1,0:T(8,128)(2,1)}) custom-call(s32[1]{0:T(128)} %bitcast.core_ref, bf16[384,1280]{1,0:T(8,128)(2,1)} %fusion.2.act_ref, bf16[576,1280]{1,0:T(8,128)(2,1)} %bitcast.7), custom_call_target="tpu_custom_call" | custom-call | flops 283115520 | bytes 4030464 | tf_op jit(solution)/shard_map/pallas_call | solution.py:35
  35.0 0.0 collective-permute-done.act_ref
  35.0 3.5 %shard_map.124 = (f32[384,288]{1,0:T(8,128)}, bf16[1280,384]{1,0:T(8,128)(2,1)}) custom-call(s32[1]{0:T(128)} %bitcast.core_ref, bf16[384,1280]{1,0:T(8,128)(2,1)} %collective-permute-done.act_ref, bf16[576,1280]{1,0:T(8,128)(2,1)} %bitcast.8), custom_call_target="tpu_custom_call" | custom-call | flops 283115520 | bytes 4030464 | tf_op jit(solution)/shard_map/pallas_call | solution.py:35
  38.5 4.7 %all-to-all-done.arrived_ref = bf16[24,72,128]{2,1,0:T(8,128)(2,1)S(1)} async-done(((bf16[24,72,128]{2,1,0:T(8,128)(2,1)}), bf16[24,72,128]{2,1,0:T(8,128)(2,1)S(1)}, u32[]{:S(2)}, u32[]{:S(2)}) %all-to-all-start) | async-done | bytes 442400 | tf_op jit(solution)/shard_map/all_to_all | solution.py:211
  43.2 0.0 copy-start.5
  43.2 0.8 copy-done.5
  43.9 4.4 %shard_map.125 = bf16[4,720,128]{2,1,0:T(8,128)(2,1)} custom-call(s32[1]{0:T(128)} %bitcast.core_ref, bf16[24,72,128]{2,1,0:T(8,128)(2,1)} %copy-done.5, f32[384,288]{1,0:T(8,128)} %get-tuple-element.11.own_pred, bf16[1280,384]{1,0:T(8,128)(2,1)} %get-tuple-element.12.own_act_t, f32[384,288]{1,0:T(8,128)} %get-tuple-element.13.other_pred, ...), custom_call_target="tpu_custom_call" | custom-call | flops 754974720 | bytes 3145728 | tf_op jit(solution)/shard_map/pallas_call | solution.py:35
  48.3 0.0 copy-start.1
  48.3 0.0 copy-start.2
  48.3 0.0 copy-start.3
  48.4 12.9 %all_to_all.20.got_ref = bf16[4,720,128]{2,1,0:T(8,128)(2,1)S(1)} all-to-all(bf16[4,720,128]{2,1,0:T(8,128)(2,1)} %shard_map.125), channel_id=1, replica_groups=mesh['z'=12,'x'=4,'y'=8,'c'=2] {'x'}, dimensions={0} | all-to-all | bytes 1474560 | tf_op jit(solution)/shard_map/all_to_all | solution.py:211
  61.3 0.2 shard_map.126
  61.5 30.6 %all_to_all.21 = bf16[96,8,128]{2,1,0:T(8,128)(2,1)S(1)} all-to-all(bf16[96,8,128]{2,1,0:T(8,128)(2,1)S(1)} %shard_map.126), channel_id=1, replica_groups=mesh['z'=12,'x'=4,'y'=8,'c'=2] {'z','y'}, dimensions={0} | all-to-all | bytes 393216 | tf_op jit(solution)/shard_map/all_to_all | solution.py:211
  92.1 0.1 convert_reduce_fusion
  92.3 16.5 %all_to_all.22.tiles_ref = f32[24,8,128]{2,1,0:T(8,128)S(1)} all-to-all(f32[24,8,128]{2,1,0:T(8,128)S(1)} %broadcast_in_dim.4), channel_id=1, replica_groups=mesh['z'=12,'x'=4,'y'=8,'c'=2] {'z','c'}, dimensions={0} | all-to-all | bytes 196608 | tf_op jit(solution)/shard_map/all_to_all | solution.py:211
  108.8 0.0 copy-done.1
  108.8 0.0 copy-done.2
  108.8 0.0 copy-done.3
  108.8 0.8 shard_map.127
  (1 shorter events, 0.0 us)
Async XLA Ops:
  0.6 1.8 %copy-start = (bf16[1152,1152]{1,0:T(8,128)(2,1)S(1)}, bf16[1152,1152]{1,0:T(8,128)(2,1)}, u32[]{:S(2)}) copy-start(bf16[1152,1152]{1,0:T(8,128)(2,1)} %param.11) | copy-start | bytes 7962628
  0.6 0.8 copy-start.4
  6.8 36.4 %all-to-all-start = ((bf16[24,72,128]{2,1,0:T(8,128)(2,1)}), bf16[24,72,128]{2,1,0:T(8,128)(2,1)S(1)}, u32[]{:S(2)}, u32[]{:S(2)}) async-start(bf16[24,72,128]{2,1,0:T(8,128)(2,1)} %shard_map.122), calls=%async_computation | async-start | bytes 884736 | tf_op jit(solution)/shard_map/all_to_all | solution.py:211
  29.5 5.5 %collective-permute-start = (bf16[384,1280]{1,0:T(8,128)(2,1)}, bf16[384,1280]{1,0:T(8,128)(2,1)}, u32[]{:S(2)}, u32[]{:S(2)}) collective-permute-start(bf16[384,1280]{1,0:T(8,128)(2,1)} %fusion.2.act_ref), channel_id=1, source_target_pairs={{0,1},{1,0},{2,3},{3,2},{4,5},{5,4},{6,7},{7,6},{8,9},{9,8},{10,11... | collective-permute-start | bytes 2949128 | tf_op jit(solution)/shard_map/ppermute | solution.py:243
  43.2 0.8 copy-start.5
  48.3 60.4 %copy-start.1 = (f32[20,576]{1,0:T(8,128)S(1)}, f32[20,576]{1,0:T(8,128)}, u32[]{:S(2)}) copy-start(f32[20,576]{1,0:T(8,128)} %master_ref.1) | copy-start | bytes 138244
  48.3 60.4 %copy-start.2 = (f32[20,576]{1,0:T(8,128)S(1)}, f32[20,576]{1,0:T(8,128)}, u32[]{:S(2)}) copy-start(f32[20,576]{1,0:T(8,128)} %one_ref.1) | copy-start | bytes 138244
  48.3 60.4 %copy-start.3 = (f32[20,576]{1,0:T(8,128)S(1)}, f32[20,576]{1,0:T(8,128)}, u32[]{:S(2)}) copy-start(f32[20,576]{1,0:T(8,128)} %two_ref.1) | copy-start | bytes 138244
where the time goes:
time: 110 us
  blocking collectives  60.1 us (55%)
  starting transfers between devices  18.8 us (17%)
  Pallas kernels  13.7 us (12%)
  other arithmetic  6.1 us (6%)
  waiting for transfers between devices  4.67 us (4%)
  matrix products  2.99 us (3%)
  local copies, waits for them, and re-layouts  2.5 us (2%)
    all_to_all x3, blocking collectives, exchange(): return lax.all_to_all(x, axis, split_axis=0, concat_axis=0, tiled=True)  60.1 us
    all_to_all x1, starting transfers between devices, exchange(): return lax.all_to_all(x, axis, split_axis=0, concat_axis=0, tiled=True)  16.7 us
    pallas_call x7, Pallas kernels, call(): pl.pallas_call(kernel, out_shape=outs, in_specs=specs or [pl.BlockSpec()]...  13.7 us
    convert_element_type x1, other arithmetic, body(): jax.nn.gelu(student_hidden.astype(f32), approximate=False).astype(bf16)  5.99 us
    all_to_all x1, waiting for transfers between devices, exchange(): return lax.all_to_all(x, axis, split_axis=0, concat_axis=0, tiled=True)  4.67 us
    dot_general x1, matrix products, body(): jnp.dot(projected, phi_rotate, preferred_element_type=f32).astype(bf16)  2.99 us
    unnamed x12, local copies, waits for them, and re-layouts  2.29 us
  transfers between devices with their start and end apart: 2, of which 1 were waited for; matrix products, arithmetic and copies ran while one was open for 5% of the time, Pallas kernels for 6%

commit v1 on v0

--- a/solution.py
+++ b/solution.py
@@ -107,17 +107,38 @@
 
 def error_kernel(
     core_ref,
+    arrived_hbm,
+    own_pred_hbm,
+    own_act_hbm,
+    other_pred_hbm,
+    other_act_hbm,
+    out_ref,
+    main_t,
+    last_t,
+    grad_last,
     arrived_ref,
     own_pred,
     own_act_t,
     other_pred,
     other_act_t,
-    out_ref,
-    main_t,
-    last_t,
-    grad_last,
+    sems,
 ):
     core = core_ref[0]
+    copies = [
+        pltpu.make_async_copy(far, near, sems.at[i])
+        for i, (far, near) in enumerate(
+            (
+                (arrived_hbm, arrived_ref),
+                (own_pred_hbm, own_pred),
+                (own_act_hbm, own_act_t),
+                (other_pred_hbm, other_pred),
+                (other_act_hbm, other_act_t),
+            )
+        )
+    ]
+    for copy in copies:
+        copy.start()
+    copies[0].wait()
 
     def scaled(pred, target):
         return (jnp.where(target < 0.1 * EMPTY, pred - target, 0.0) / DW).astype(bf16)
@@ -134,6 +155,9 @@
             main_t[at : at + CAP, 128:256] = block[32:64]
             for q in range(4):
                 last_t[at + 8 * q : at + 8 * q + 8, :] = turn(block[64:72], -32 * q)
+        first = 1 if pred is own_pred else 3
+        copies[first].wait()
+        copies[first + 1].wait()
         units = act_t[...]
         main_part = jnp.dot(units, scaled(pred[:, :256], main_t[...]), preferred_element_type=f32)
         last_part = jnp.dot(units, scaled(pred[:, 256:], last_t[:, :32]), preferred_element_type=f32)
@@ -257,12 +281,18 @@
         error_kernel,
         shape((NX, XROWS, 128), bf16),
         (core, arrived, *student(activated), *student(other)),
-        specs=[scalar] + [whole] * 5,
+        specs=[scalar] + [pl.BlockSpec(memory_space=pltpu.HBM)] * 5,
         vmem=60,
         scratch=(
             pltpu.VMEM((SLOTS, 256), f32),
             pltpu.VMEM((SLOTS, 128), f32),
             pltpu.VMEM((H, 128), f32),
+            pltpu.VMEM((NZ * NC, PACKED, 128), bf16),
+            pltpu.VMEM((SLOTS, 288), f32),
+            pltpu.VMEM((H, SLOTS), bf16),
+            pltpu.VMEM((SLOTS, 288), f32),
+            pltpu.VMEM((H, SLOTS), bf16),
+            pltpu.SemaphoreType.DMA((5,)),
         ),
         flops=4 * SLOTS * H * 384,
         moved=4 * SLOTS * H + 8 * SLOTS * 384,

time: 110 us -> 110 us (level)
  no operation moved by 1% of the time
where the time goes in v1:
time: 110 us; the launch traced here: 109 us
  blocking collectives  59.7 us (54%)
  starting transfers between devices  18.8 us (17%)
  Pallas kernels  13.8 us (13%)
  other arithmetic  6.1 us (6%)
  waiting for transfers between devices  4.67 us (4%)
  matrix products  2.99 us (3%)
  local copies, waits for them, and re-layouts  2.51 us (2%)
    all_to_all x3, blocking collectives, exchange(): return lax.all_to_all(x, axis, split_axis=0, concat_axis=0, tiled=True)  59.7 us
    all_to_all x1, starting transfers between devices, exchange(): return lax.all_to_all(x, axis, split_axis=0, concat_axis=0, tiled=True)  16.7 us
    pallas_call x7, Pallas kernels, call(): pl.pallas_call(kernel, out_shape=outs, in_specs=specs or [pl.BlockSpec()]...  13.8 us
    convert_element_type x1, other arithmetic, body(): jax.nn.gelu(student_hidden.astype(f32), approximate=False).astype(bf16)  5.99 us
    all_to_all x1, waiting for transfers between devices, exchange(): return lax.all_to_all(x, axis, split_axis=0, concat_axis=0, tiled=True)  4.67 us
    dot_general x1, matrix products, body(): jnp.dot(projected, phi_rotate, preferred_element_type=f32).astype(bf16)  2.99 us
    unnamed x12, local copies, waits for them, and re-layouts  2.3 us
  transfers between devices with their start and end apart: 2, of which 1 were waited for; matrix products, arithmetic and copies ran while one was open for 5% of the time, Pallas kernels for 6%

profile of v1, /device:TPU:1, one launch (start us, length us, event | category | flops | bytes accessed | tf_op | source)
XLA Modules:
  0.0 109.2 jit_solution(5586453905500231)
XLA Ops:
  0.6 0.0 copy-start
  0.6 0.0 copy-start.4
  0.7 0.8 copy-done.4
  1.5 0.2 shard_map.121.place_ref
  1.7 0.7 copy-done
  2.4 3.0 %convolution_convert_fusion = bf16[256,576]{0,1:T(8,128)(2,1)S(1)} fusion(bf16[1152,576]{0,1:T(8,128)(2,1)} %param.13, bf16[256,1152]{1,0:T(8,128)(2,1)} %param.10, bf16[1152,1152]{1,0:T(8,128)(2,1)S(1)} %copy-done, f32[1152]{0:T(1024)} %param.12), kind=kOutput, calls=%fused_computation.36 | convolution fusion | flops 1019953152 | bytes 4870656 | tf_op jit(solution)/shard_map/dot_general | solution.py:256
  5.4 0.2 copy.14.rows_ref
  5.6 1.2 %shard_map.122 = bf16[24,72,128]{2,1,0:T(8,128)(2,1)} custom-call(bf16[384,256]{1,0:T(8,128)(2,1)S(1)} %shard_map.121.place_ref, bf16[256,576]{1,0:T(8,128)(2,1)S(1)} %copy.14.rows_ref), custom_call_target="tpu_custom_call" | custom-call | flops 125829120 | bytes 819200 | tf_op jit(solution)/shard_map/pallas_call | solution.py:35
  6.8 16.7 %all-to-all-start = ((bf16[24,72,128]{2,1,0:T(8,128)(2,1)}), bf16[24,72,128]{2,1,0:T(8,128)(2,1)S(1)}, u32[]{:S(2)}, u32[]{:S(2)}) async-start(bf16[24,72,128]{2,1,0:T(8,128)(2,1)} %shard_map.122), calls=%async_computation | async-start | bytes 884736 | tf_op jit(solution)/shard_map/all_to_all | solution.py:235
  23.5 6.0 %fusion.2.act_ref = bf16[384,1280]{1,0:T(8,128)(2,1)} fusion(bf16[384,1280]{1,0:T(8,128)(2,1)} %param.15), kind=kLoop, calls=%fused_computation.6 | loop fusion | flops 32440320 | bytes 1966080 | tf_op jit(solution)/shard_map/convert_element_type | solution.py:266
  29.5 2.1 %collective-permute-start = (bf16[384,1280]{1,0:T(8,128)(2,1)}, bf16[384,1280]{1,0:T(8,128)(2,1)}, u32[]{:S(2)}, u32[]{:S(2)}) collective-permute-start(bf16[384,1280]{1,0:T(8,128)(2,1)} %fusion.2.act_ref), channel_id=1, source_target_pairs={{0,1},{1,0},{2,3},{3,2},{4,5},{5,4},{6,7},{7,6},{8,9},{9,8},{10,11... | collective-permute-start | bytes 2949128 | tf_op jit(solution)/shard_map/ppermute | solution.py:267
  31.6 3.5 %shard_map.123 = (f32[384,288]{1,0:T(8,128)}, bf16[1280,384]{1,0:T(8,128)(2,1)}) custom-call(s32[1]{0:T(128)} %bitcast.core_ref, bf16[384,1280]{1,0:T(8,128)(2,1)} %fusion.2.act_ref, bf16[576,1280]{1,0:T(8,128)(2,1)} %bitcast.7), custom_call_target="tpu_custom_call" | custom-call | flops 283115520 | bytes 4030464 | tf_op jit(solution)/shard_map/pallas_call | solution.py:35
  35.0 0.0 collective-permute-done.act_ref
  35.0 3.5 %shard_map.124 = (f32[384,288]{1,0:T(8,128)}, bf16[1280,384]{1,0:T(8,128)(2,1)}) custom-call(s32[1]{0:T(128)} %bitcast.core_ref, bf16[384,1280]{1,0:T(8,128)(2,1)} %collective-permute-done.act_ref, bf16[576,1280]{1,0:T(8,128)(2,1)} %bitcast.8), custom_call_target="tpu_custom_call" | custom-call | flops 283115520 | bytes 4030464 | tf_op jit(solution)/shard_map/pallas_call | solution.py:35
  38.5 4.7 %all-to-all-done.arrived_hbm = bf16[24,72,128]{2,1,0:T(8,128)(2,1)S(1)} async-done(((bf16[24,72,128]{2,1,0:T(8,128)(2,1)}), bf16[24,72,128]{2,1,0:T(8,128)(2,1)S(1)}, u32[]{:S(2)}, u32[]{:S(2)}) %all-to-all-start) | async-done | bytes 442400 | tf_op jit(solution)/shard_map/all_to_all | solution.py:235
  43.2 0.0 copy-start.5
  43.2 0.8 copy-done.5
  43.9 4.4 %shard_map.125 = bf16[4,720,128]{2,1,0:T(8,128)(2,1)} custom-call(s32[1]{0:T(128)} %bitcast.core_ref, bf16[24,72,128]{2,1,0:T(8,128)(2,1)} %copy-done.5, f32[384,288]{1,0:T(8,128)} %get-tuple-element.11.own_pred_hbm, bf16[1280,384]{1,0:T(8,128)(2,1)} %get-tuple-element.12.own_act_hbm, f32[384,288]{1,0:T(8,128)} %get-tuple-element.13.other_pred_hbm, ...), custom_call_target="tpu_custom_call" | custom-call | flops 754974720 | bytes 3145728 | tf_op jit(solution)/shard_map/pallas_call | solution.py:35
  48.4 0.0 copy-start.1
  48.4 0.0 copy-start.2
  48.4 0.0 copy-start.3
  48.4 12.9 %all_to_all.20.got_ref = bf16[4,720,128]{2,1,0:T(8,128)(2,1)S(1)} all-to-all(bf16[4,720,128]{2,1,0:T(8,128)(2,1)} %shard_map.125), channel_id=1, replica_groups=mesh['z'=12,'x'=4,'y'=8,'c'=2] {'x'}, dimensions={0} | all-to-all | bytes 1474560 | tf_op jit(solution)/shard_map/all_to_all | solution.py:235
  61.3 0.2 shard_map.126
  61.6 30.2 %all_to_all.21 = bf16[96,8,128]{2,1,0:T(8,128)(2,1)S(1)} all-to-all(bf16[96,8,128]{2,1,0:T(8,128)(2,1)S(1)} %shard_map.126), channel_id=1, replica_groups=mesh['z'=12,'x'=4,'y'=8,'c'=2] {'z','y'}, dimensions={0} | all-to-all | bytes 393216 | tf_op jit(solution)/shard_map/all_to_all | solution.py:235
  91.7 0.1 convert_reduce_fusion
  91.8 16.6 %all_to_all.22.tiles_ref = f32[24,8,128]{2,1,0:T(8,128)S(1)} all-to-all(f32[24,8,128]{2,1,0:T(8,128)S(1)} %broadcast_in_dim.4), channel_id=1, replica_groups=mesh['z'=12,'x'=4,'y'=8,'c'=2] {'z','c'}, dimensions={0} | all-to-all | bytes 196608 | tf_op jit(solution)/shard_map/all_to_all | solution.py:235
  108.5 0.0 copy-done.1
  108.5 0.0 copy-done.2
  108.5 0.0 copy-done.3
  108.5 0.8 shard_map.127
  (1 shorter events, 0.0 us)
Async XLA Ops:
  0.6 1.8 %copy-start = (bf16[1152,1152]{1,0:T(8,128)(2,1)S(1)}, bf16[1152,1152]{1,0:T(8,128)(2,1)}, u32[]{:S(2)}) copy-start(bf16[1152,1152]{1,0:T(8,128)(2,1)} %param.11) | copy-start | bytes 7962628
  0.6 0.8 copy-start.4
  6.8 36.4 %all-to-all-start = ((bf16[24,72,128]{2,1,0:T(8,128)(2,1)}), bf16[24,72,128]{2,1,0:T(8,128)(2,1)S(1)}, u32[]{:S(2)}, u32[]{:S(2)}) async-start(bf16[24,72,128]{2,1,0:T(8,128)(2,1)} %shard_map.122), calls=%async_computation | async-start | bytes 884736 | tf_op jit(solution)/shard_map/all_to_all | solution.py:235
  29.5 5.5 %collective-permute-start = (bf16[384,1280]{1,0:T(8,128)(2,1)}, bf16[384,1280]{1,0:T(8,128)(2,1)}, u32[]{:S(2)}, u32[]{:S(2)}) collective-permute-start(bf16[384,1280]{1,0:T(8,128)(2,1)} %fusion.2.act_ref), channel_id=1, source_target_pairs={{0,1},{1,0},{2,3},{3,2},{4,5},{5,4},{6,7},{7,6},{8,9},{9,8},{10,11... | collective-permute-start | bytes 2949128 | tf_op jit(solution)/shard_map/ppermute | solution.py:267
  43.2 0.8 copy-start.5
  48.4 60.1 %copy-start.1 = (f32[20,576]{1,0:T(8,128)S(1)}, f32[20,576]{1,0:T(8,128)}, u32[]{:S(2)}) copy-start(f32[20,576]{1,0:T(8,128)} %master_ref.1) | copy-start | bytes 138244
  48.4 60.1 %copy-start.2 = (f32[20,576]{1,0:T(8,128)S(1)}, f32[20,576]{1,0:T(8,128)}, u32[]{:S(2)}) copy-start(f32[20,576]{1,0:T(8,128)} %one_ref.1) | copy-start | bytes 138244
  48.4 60.1 %copy-start.3 = (f32[20,576]{1,0:T(8,128)S(1)}, f32[20,576]{1,0:T(8,128)}, u32[]{:S(2)}) copy-start(f32[20,576]{1,0:T(8,128)} %two_ref.1) | copy-start | bytes 138244
